TPU v7x, 32 devices: a whole 2x2x4 slice. The times are simulated.
32 devices in a mesh: pitch: 2 (over core), axial: 4 (over y, x), span: 4 (over z).
Axes of the slice: x: 2, y: 2, z: 4, core: 2. Of those that a mesh axis runs over, the one named last changes fastest.
Arguments:
- state: float32 [5, 16, 128, 512], P(None, 'pitch', 'axial', 'span'), as said below
- coeffs: float32 [2, 4, 5, 128, 512], P(None, None, None, 'axial', 'span'), may hold values from -3 to 3
- lag_shift: int32 [1], replicated, may hold values from 0 to 63
- harmonics: int32 [512], P('span'), may hold values from 1 to 4
Outputs:
- new_state: float32 [5, 16, 128, 512], P(None, 'pitch', 'axial', 'span')
Inputs may be any that keep to these rules, and one draw needn't show every extreme that they name: `state`: density lies in 0.8 to 1.25, momenta within -1.5 to 1.5, total energy within 1.6 to 3.4.
All inputs are finite; a program needn't handle non-finite values.
Results may differ from a plain program's by a relative error of at most 0.0001.
Values sent between devices are 32-bit elements; how exact they have to be, the bound alone decides.
A program may use at most 64 MiB of HBM per device.

v0:
```python
import math

import jax
import jax.numpy as jnp
from jax import lax
from jax.sharding import PartitionSpec as P

HARM_MAX = 4
PERIOD_SAMPLES = 64


HEAT_RATIO_GAS = 1.4
STEP_RATE = 0.25
DAMPING = 0.5
STENCIL = (1.0, -8.0, 28.0, -56.0, 70.0, -56.0, 28.0, -8.0, 1.0)


def padded(cells, sides, width, closed):
    for axis, dim in sides:
        count = lax.axis_size(axis)
        ends = count if closed else count - 1
        head = lax.slice_in_dim(cells, 0, width, axis=dim)
        tail = lax.slice_in_dim(cells, cells.shape[dim] - width, cells.shape[dim], axis=dim)
        cells = jnp.concatenate(
            [
                lax.ppermute(tail, axis, [(i, (i + 1) % count) for i in range(ends)]),
                cells,
                lax.ppermute(head, axis, [((i + 1) % count, i) for i in range(ends)]),
            ],
            axis=dim,
        )
    return cells


def pitch_flux(state):
    density = state[0]
    speed = state[2] / density
    kinetic = 0.5 * (state[1] * state[1] + state[2] * state[2] + state[3] * state[3]) / density
    pressure = (HEAT_RATIO_GAS - 1.0) * (state[4] - kinetic)
    return jnp.stack(
        [
            state[2],
            state[1] * speed,
            state[2] * speed + pressure,
            state[3] * speed,
            (state[4] + pressure) * speed,
        ]
    )


def seam_jump(coeffs, lag_shift, harmonics):
    order = jnp.arange(HARM_MAX)
    phase = (
        2.0
        * math.pi
        / PERIOD_SAMPLES
        * (order + 1).astype(jnp.float32)
        * lag_shift[0].astype(jnp.float32)
    )
    active = (order[:, None] < harmonics[None, :]).astype(jnp.float32)
    cosine = active * jnp.cos(phase)[:, None]
    sine = active * jnp.sin(phase)[:, None]
    first = jnp.sum(cosine[:, None, None, :] * coeffs[0], axis=0)
    second = jnp.sum(sine[:, None, None, :] * coeffs[1], axis=0)
    return first + second


def damping_from(extended, naxial, nspan):
    along = jnp.zeros_like(extended[:, :, 4 : 4 + naxial, 4 : 4 + nspan])
    across = jnp.zeros_like(along)
    for displacement in range(9):
        along = (
            along
            + STENCIL[displacement]
            * extended[:, :, displacement : displacement + naxial, 4 : 4 + nspan]
        )
        across = (
            across
            + STENCIL[displacement]
            * extended[:, :, 4 : 4 + naxial, displacement : displacement + nspan]
        )
    return (along + across) / 256.0


def signed_power(base, count):
    magnitude = jnp.power(jnp.float32(abs(base)), jnp.asarray(count).astype(jnp.float32))
    if base < 0.0:
        magnitude = magnitude * (1 - 2 * (jnp.asarray(count) % 2)).astype(jnp.float32)
    return magnitude


def line_root(main_band_coefficient, neighbour_band_coefficient):
    characteristic_polynomial_radicand = math.sqrt(
        main_band_coefficient * main_band_coefficient
        - 4.0 * neighbour_band_coefficient * neighbour_band_coefficient
    )
    recurrence_decay_number = (-main_band_coefficient + characteristic_polynomial_radicand) / (
        2.0 * neighbour_band_coefficient
    )
    return (
        recurrence_decay_number,
        1.0 / (main_band_coefficient + 2.0 * neighbour_band_coefficient * recurrence_decay_number),
    )


def edge_sums(values, recurrence_decay_number):
    pitch_cells = values.shape[1]
    cell_pos = jnp.arange(pitch_cells)
    tail_part = jnp.einsum(
        "j,fjas->fas",
        signed_power(recurrence_decay_number, pitch_cells - 1 - cell_pos),
        values,
        precision=lax.Precision.HIGHEST,
    )
    head_part = jnp.einsum(
        "j,fjas->fas",
        signed_power(recurrence_decay_number, cell_pos),
        values,
        precision=lax.Precision.HIGHEST,
    )
    return (tail_part, head_part)


def factor_root_weights(step_decays, count):
    return jnp.stack(
        [signed_power(step_decays[0], count), signed_power(step_decays[1], count)], axis=-1
    )


def finish(values, recurrence_decay_number, scale_value, carry_up, carry_down):
    pitch_cells = values.shape[1]
    cell_pos = jnp.arange(pitch_cells)
    kernel = signed_power(recurrence_decay_number, jnp.abs(cell_pos[:, None] - cell_pos[None, :]))
    solved = jnp.einsum("ij,fjas->fias", kernel, values, precision=lax.Precision.HIGHEST)
    enter_weights = signed_power(recurrence_decay_number, cell_pos + 1)
    leave_weights = signed_power(recurrence_decay_number, pitch_cells - cell_pos)
    solved = (
        solved
        + enter_weights[None, :, None, None] * carry_up[:, None]
        + leave_weights[None, :, None, None] * carry_down[:, None]
    )
    return scale_value * solved


def shards(state, coeffs, lag_shift, harmonics):
    flux = pitch_flux(state)
    jump = seam_jump(coeffs, lag_shift, harmonics)
    npitch = lax.axis_size("pitch")
    position = lax.axis_index("pitch")
    at_first = jnp.where(position == 0, 1.0, 0.0).astype(jnp.float32)
    at_last = jnp.where(position == npitch - 1, 1.0, 0.0).astype(jnp.float32)
    widened = padded(flux, (("pitch", 1),), 1, True)
    rhs = 0.75 * (widened[:, 2:] - widened[:, :-2])
    rhs = rhs.at[:, 0].add(0.75 * (at_first * jump))
    rhs = rhs.at[:, -1].add(0.75 * (at_last * jump))
    pitch_cells = rhs.shape[1]
    pitch_total = pitch_cells * npitch
    diffusion = float(pitch_total * pitch_total // 64)
    compact_root, compact_scale = line_root(1.0, 0.25)
    relax_root, relax_scale = line_root(1.0 + 2.0 * diffusion, -diffusion)
    tail_compact, head_compact = edge_sums(rhs, compact_root)
    tail_relax, head_relax = edge_sums(state, relax_root)
    tail_sums = jnp.stack([tail_compact, tail_relax])
    leading_partial_totals = jnp.stack([head_compact, head_relax])
    step_decays = (compact_root**pitch_cells, relax_root**pitch_cells)
    wrap_factors = jnp.array(
        [1.0 / (1.0 - step_decays[0] ** npitch), 1.0 / (1.0 - step_decays[1] ** npitch)],
        jnp.float32,
    )
    collected = (
        lax.all_gather(tail_sums[None], "pitch", axis=0, tiled=True),
        lax.all_gather(leading_partial_totals[None], "pitch", axis=0, tiled=True),
    )
    others = jnp.arange(npitch)
    up_weights = (
        factor_root_weights(step_decays, (position - 1 - others) % npitch) * wrap_factors[None, :]
    )
    descending_sweep_multipliers = (
        factor_root_weights(step_decays, (others - position - 1) % npitch) * wrap_factors[None, :]
    )
    carry_up = jnp.einsum(
        "er,erfas->rfas", up_weights, collected[0], precision=lax.Precision.HIGHEST
    )
    carry_down = jnp.einsum(
        "er,erfas->rfas",
        descending_sweep_multipliers,
        collected[1],
        precision=lax.Precision.HIGHEST,
    )
    deriv = finish(rhs, compact_root, compact_scale, carry_up[0], carry_down[0])
    smoothed_increment = finish(state, relax_root, relax_scale, carry_up[1], carry_down[1])
    extended = padded(state, (("axial", 2), ("span", 3)), 4, False)
    damp = damping_from(extended, state.shape[2], state.shape[3])
    return smoothed_increment - STEP_RATE * deriv - DAMPING * damp


def solution(mesh):
    placed = (
        P(None, "pitch", "axial", "span"),
        P(None, None, None, "axial", "span"),
        P(),
        P("span"),
    )
    return jax.shard_map(
        shards,
        mesh=mesh,
        in_specs=placed,
        out_specs=P(None, "pitch", "axial", "span"),
        check_vma=False,
    )
```

profile of v0, /device:TPU:0, one launch (start us, length us, event | category | flops | bytes accessed | tf_op | source)
XLA Modules:
  0.0 46.5 jit_solution(12623928123771898618)
XLA Ops:
  0.0 1.0 %slice_dynamic-update-slice_fusion = f32[5,8,32,128]{3,2,1,0:T(8,128)S(1)} fusion(f32[5,8,32,128]{3,2,1,0:T(8,128)} %param.9), kind=kLoop, calls=%fused_computation.85 | loop fusion | bytes 262144
  1.0 1.1 %multiply_dynamic-update-slice_fusion.2 = (f32[5,8,32,128]{3,2,1,0:T(8,128)S(1)}, f32[1,8,32,128]{3,2,1,0:T(8,128)S(1)}) fusion(f32[5,8,32,128]{3,2,1,0:T(8,128)S(1)} %slice_dynamic-update-slice_fusion, f32[5,8,32,128]{3,2,1,0:T(8,128)} %param.9), kind=kLoop, calls=%fused_computation.83 | loop fusion | flops 65536 | bytes 655360
  2.1 0.0 copy-done
  2.1 0.1 add_dynamic-update-slice_fusion
  2.2 0.6 %collective-permute-start = (f32[5,1,32,128]{3,2,1,0:T(8,128)S(1)}, f32[5,1,32,128]{3,2,1,0:T(8,128)S(1)}, u32[]{:S(2)}, u32[]{:S(2)}) collective-permute-start(f32[5,1,32,128]{3,2,1,0:T(8,128)S(1)} %get-tuple-element.37), channel_id=1, source_target_pairs={{16,0},{0,16},{17,1},{1,17},{18,2},{2,18},{19,3},{3,19},{20,4},{4,... | collective-permute-start | bytes 245768 | tf_op jit(solution)/shard_map/ppermute | solution.py:28
  2.8 0.1 collective-permute-start.1
  2.9 4.8 %collective-permute-start.2 = (f32[5,8,4,128]{3,1,2,0:T(8,128)S(1)}, f32[5,8,4,128]{3,1,2,0:T(8,128)S(1)}, u32[]{:S(2)}, u32[]{:S(2)}) collective-permute-start(f32[5,8,4,128]{3,1,2,0:T(8,128)S(1)} %copy.68), channel_id=1, source_target_pairs={{0,4},{4,8},{8,12},{1,5},{5,9},{9,13},{2,6},{6,10},{10,14},{3,7},{... | collective-permute-start | bytes 245768 | tf_op jit(solution)/shard_map/ppermute | solution.py:26
  7.7 0.0 copy-start.4
  7.8 0.0 copy-start.3
  7.8 0.0 copy-start.1
  7.8 1.4 %collective-permute-start.3 = (f32[5,8,4,128]{3,1,2,0:T(8,128)S(1)}, f32[5,8,4,128]{3,1,2,0:T(8,128)S(1)}, u32[]{:S(2)}, u32[]{:S(2)}) collective-permute-start(f32[5,8,4,128]{3,1,2,0:T(8,128)S(1)} %copy.69), channel_id=1, source_target_pairs={{4,0},{8,4},{12,8},{5,1},{9,5},{13,9},{6,2},{10,6},{14,10},{7,3},{... | collective-permute-start | bytes 245768 | tf_op jit(solution)/shard_map/ppermute | solution.py:28
  9.2 1.0 %fusion.111 = f32[1,5,32,128]{3,0,2,1:T(1,128)S(1)} fusion(f32[5,8,32,128]{3,2,1,0:T(8,128)S(1)} %copy-done), kind=kOutput, calls=%fused_computation.179 | convolution fusion | flops 1966096 | bytes 737280 | tf_op jit(solution)/shard_map/j,fjas->fas/dot_general | solution.py:109
  10.2 1.0 %fusion.88 = f32[1,5,32,128]{3,0,2,1:T(1,128)S(1)} fusion(f32[5,8,32,128]{3,2,1,0:T(8,128)S(1)} %copy-done), kind=kOutput, calls=%fused_computation.159 | convolution fusion | flops 1966088 | bytes 737280 | tf_op jit(solution)/shard_map/j,fjas->fas/dot_general | solution.py:115
  12.0 0.0 copy-done.4
  12.0 0.1 fusion.82
  12.0 0.1 copy.37
  12.1 0.1 copy.44
  12.2 0.0 copy-done.3
  12.2 0.1 fusion.76
  12.3 0.0 copy-done.1
  12.3 0.1 fusion.44
  12.4 0.0 collective-permute-done
  12.4 0.0 collective-permute-done.1
  12.4 0.1 fusion.38
  12.6 1.0 %fusion.41 = f32[1,5,32,128]{3,0,2,1:T(1,128)S(1)} fusion(f32[5,8,32,128]{3,2,1,0:T(8,128)S(1)} %fusion.50), kind=kOutput, calls=%fused_computation.66 | convolution fusion | flops 1966216 | bytes 737280 | tf_op jit(solution)/shard_map/j,fjas->fas/dot_general | solution.py:109
  13.6 1.0 %fusion.39 = f32[1,5,32,128]{3,0,2,1:T(1,128)S(1)} fusion(f32[5,8,32,128]{3,2,1,0:T(8,128)S(1)} %fusion.50), kind=kOutput, calls=%fused_computation.64 | convolution fusion | flops 1966168 | bytes 737280 | tf_op jit(solution)/shard_map/j,fjas->fas/dot_general | solution.py:115
  14.6 2.0 %all-gather = f32[4,5,32,128]{3,2,1,0:T(8,128)S(1)} all-gather(f32[2,5,32,128]{3,2,1,0:T(8,128)S(1)} %pad_maximum_fusion.4), channel_id=2, replica_groups=mesh['pitch'=2,'axial'=4,'span'=4] {'pitch'}, dimensions={0}, use_global_device_ids=true | all-gather | bytes 491520 | tf_op jit(solution)/shard_map/all_gather | solution.py:171
  16.6 2.0 %all-gather.1 = f32[4,5,32,128]{3,2,1,0:T(8,128)S(1)} all-gather(f32[2,5,32,128]{3,2,1,0:T(8,128)S(1)} %pad_maximum_fusion.5), channel_id=3, replica_groups=mesh['pitch'=2,'axial'=4,'span'=4] {'pitch'}, dimensions={0}, use_global_device_ids=true | all-gather | bytes 491520 | tf_op jit(solution)/shard_map/all_gather | solution.py:172
  18.7 1.3 %fusion.48 = f32[2,1,5,32,128]{4,1,3,2,0:T(1,128)S(1)} fusion(f32[2,2,1,1,1]{0,2,4,3,1:T(1,128)S(1)} %copy.37, f32[2,2,5,32,128]{4,3,2,1,0:T(8,128)S(1)} %bitcast.111), kind=kOutput, calls=%fused_computation.75 | convolution fusion | flops 983040 | bytes 491536 | tf_op jit(solution)/shard_map/er,erfas->rfas/dot_general | solution.py:181
  20.0 1.3 %fusion.46 = f32[2,1,5,32,128]{4,1,3,2,0:T(1,128)S(1)} fusion(f32[2,2,1,1,1]{0,2,4,3,1:T(1,128)S(1)} %copy.44, f32[2,2,5,32,128]{4,3,2,1,0:T(8,128)S(1)} %bitcast.112), kind=kOutput, calls=%fused_computation.73 | convolution fusion | flops 983040 | bytes 491536 | tf_op jit(solution)/shard_map/er,erfas->rfas/dot_general | solution.py:184
  21.3 0.0 collective-permute-done.2
  21.3 0.6 %constant_dynamic-update-slice_fusion.1 = (f32[5,8,36,128]{3,1,2,0:T(8,128)}, f32[5,8,40,128]{3,1,2,0:T(8,128)S(1)}) fusion(f32[5,8,4,128]{3,1,2,0:T(8,128)S(1)} %collective-permute-done.2), kind=kLoop, calls=%fused_computation.97 | loop fusion | bytes 245760
  22.0 1.6 %constant_dynamic-update-slice_fusion = (f32[5,8,36,128]{3,1,2,0:T(8,128)}, f32[5,8,36,128]{3,1,2,0:T(8,128)}, f32[5,8,40,128]{3,1,2,0:T(8,128)S(1)}) fusion(f32[5,8,36,128]{3,1,2,0:T(8,128)} %get-tuple-element.48, f32[5,8,32,128]{3,2,1,0:T(8,128)S(1)} %copy-done, f32[5,8,40,128]{3,1,2,0:T(8,128)S(1)} %get-tuple-element.49), kind=kLoop, calls=%fused_computation.96 | loop fusion | bytes 2621440 | tf_op jit(solution)/shard_map/concatenate | solution.py:24
  23.6 0.0 collective-permute-done.3
  23.6 0.6 %constant_dynamic-update-slice_fusion.2 = (f32[5,8,36,128]{3,1,2,0:T(8,128)}, f32[5,8,40,128]{3,1,2,0:T(8,128)S(1)}) fusion(f32[5,8,36,128]{3,1,2,0:T(8,128)} %get-tuple-element.40, f32[5,8,4,128]{3,1,2,0:T(8,128)S(1)} %collective-permute-done.3, f32[5,8,40,128]{3,1,2,0:T(8,128)S(1)} %get-tuple-element.41), kind=kLoop, calls=%fused_computation.98 | loop fusion | bytes 245760 | tf_op jit(solution)/shard_map/concatenate | solution.py:24
  24.3 1.2 %fusion.152 = (f32[5,8,40,4]{3,1,2,0:T(8,128)}, f32[5,8,40,4]{3,1,2,0:T(8,128)S(1)}) fusion(f32[5,8,40,128]{3,1,2,0:T(8,128)S(1)} %get-tuple-element.51), kind=kLoop, calls=%fused_computation.227 | loop fusion | bytes 102400 | tf_op jit(solution)/shard_map/slice | solution.py:23
  25.4 1.5 %copy.27 = f32[5,8,40,4]{2,1,3,0:T(8,128)S(1)} copy(f32[5,8,40,4]{3,1,2,0:T(8,128)} %get-tuple-element.35) | data formatting | bytes 51200 | tf_op jit(solution)/shard_map/slice | solution.py:23
  26.9 3.5 %collective-permute-start.4 = (f32[5,8,40,4]{2,1,3,0:T(8,128)S(1)}, f32[5,8,40,4]{2,1,3,0:T(8,128)S(1)}, u32[]{:S(2)}, u32[]{:S(2)}) collective-permute-start(f32[5,8,40,4]{2,1,3,0:T(8,128)S(1)} %copy.27), channel_id=1, source_target_pairs={{0,1},{1,2},{2,3},{4,5},{5,6},{6,7},{8,9},{9,10},{10,11},{12,13},{... | collective-permute-start | bytes 76808 | tf_op jit(solution)/shard_map/ppermute | solution.py:26
  30.4 0.4 copy.29
  30.8 1.5 %collective-permute-start.5 = (f32[5,8,40,4]{2,1,3,0:T(8,128)S(1)}, f32[5,8,40,4]{2,1,3,0:T(8,128)}, u32[]{:S(2)}, u32[]{:S(2)}) collective-permute-start(f32[5,8,40,4]{2,1,3,0:T(8,128)S(1)} %copy.29), channel_id=1, source_target_pairs={{1,0},{2,1},{3,2},{5,4},{6,5},{7,6},{9,8},{10,9},{11,10},{13,12},{... | collective-permute-start | bytes 76808 | tf_op jit(solution)/shard_map/ppermute | solution.py:28
  32.2 2.0 %fusion.6 = f32[5,8,32,128]{3,1,2,0:T(8,128)} fusion(f32[5,8,32,128]{3,2,1,0:T(8,128)S(1)} %fusion.50, f32[5,32,128]{2,1,0:T(8,128)S(1)} %get-tuple-element.47, f32[8]{0:T(128)S(1)} %get-tuple-element.59, f32[5,32,128]{2,1,0:T(8,128)S(1)} %get-tuple-element.45, f32[8]{0:T(128)S(1)} %get-tuple-element.58), kind=kOutput, calls=%fused_computation.20 | convolution fusion | flops 16548992 | bytes 1474624 | tf_op jit(solution)/shard_map/ij,fjas->fias/dot_general | solution.py:134
  34.2 0.0 collective-permute-done.4
  34.2 0.4 copy.28
  34.6 2.6 %collective-permute-done.5 = f32[5,8,40,4]{2,1,3,0:T(8,128)} collective-permute-done((f32[5,8,40,4]{2,1,3,0:T(8,128)S(1)}, f32[5,8,40,4]{2,1,3,0:T(8,128)}, u32[]{:S(2)}, u32[]{:S(2)}) %collective-permute-start.5) | collective-permute-done | bytes 25632 | tf_op jit(solution)/shard_map/ppermute | solution.py:28
  37.2 2.1 %copy.30 = f32[5,8,40,4]{3,1,2,0:T(8,128)} copy(f32[5,8,40,4]{2,1,3,0:T(8,128)} %collective-permute-done.5) | data formatting | bytes 51200 | tf_op jit(solution)/shard_map/ppermute | solution.py:28
  39.3 0.0 copy-done.2
  39.3 6.2 %fusion.13 = f32[5,8,32,128]{3,1,2,0:T(8,128)S(1)} fusion(f32[5,8,40,128]{3,1,2,0:T(8,128)S(1)} %get-tuple-element.51, f32[5,8,40,4]{3,1,2,0:T(8,128)} %copy.30, f32[5,8,40,4]{3,1,2,0:T(8,128)S(1)} %copy.28, f32[5,8,36,128]{3,1,2,0:T(8,128)} %get-tuple-element.50, f32[5,8,36,128]{3,1,2,0:T(8,128)} %get-tuple-element.39, ...), kind=kOutput, calls=%fused_computation.27 | convolution fusion | flops 23265472 | bytes 9693184 | tf_op jit(solution)/shard_map/ij,fjas->fias/dot_general | solution.py:134
  45.5 1.0 %copy.31 = f32[5,8,32,128]{3,2,1,0:T(8,128)} copy(f32[5,8,32,128]{3,1,2,0:T(8,128)S(1)} %fusion.13) | data formatting | bytes 1310720 | tf_op jit(solution)/shard_map/sub | solution.py:194
  (19 shorter events, 0.3 us)
Async XLA Ops:
  0.0 2.1 %copy-start = (f32[5,8,32,128]{3,2,1,0:T(8,128)S(1)}, f32[5,8,32,128]{3,2,1,0:T(8,128)}, u32[]{:S(2)}) copy-start(f32[5,8,32,128]{3,2,1,0:T(8,128)} %param.9) | copy-start | bytes 1966084
  2.2 10.2 %collective-permute-start = (f32[5,1,32,128]{3,2,1,0:T(8,128)S(1)}, f32[5,1,32,128]{3,2,1,0:T(8,128)S(1)}, u32[]{:S(2)}, u32[]{:S(2)}) collective-permute-start(f32[5,1,32,128]{3,2,1,0:T(8,128)S(1)} %get-tuple-element.37), channel_id=1, source_target_pairs={{16,0},{0,16},{17,1},{1,17},{18,2},{2,18},{19,3},{3,19},{20,4},{4,... | collective-permute-start | bytes 245768 | tf_op jit(solution)/shard_map/ppermute | solution.py:28
  2.8 9.6 %collective-permute-start.1 = (f32[5,1,32,128]{3,2,1,0:T(8,128)S(1)}, f32[5,1,32,128]{3,2,1,0:T(8,128)S(1)}, u32[]{:S(2)}, u32[]{:S(2)}) collective-permute-start(f32[5,1,32,128]{3,2,1,0:T(8,128)S(1)} %get-tuple-element.38), channel_id=1, source_target_pairs={{0,16},{16,0},{1,17},{17,1},{2,18},{18,2},{3,19},{19,3},{4,20},{20... | collective-permute-start | bytes 245768 | tf_op jit(solution)/shard_map/ppermute | solution.py:26
  2.9 18.4 %collective-permute-start.2 = (f32[5,8,4,128]{3,1,2,0:T(8,128)S(1)}, f32[5,8,4,128]{3,1,2,0:T(8,128)S(1)}, u32[]{:S(2)}, u32[]{:S(2)}) collective-permute-start(f32[5,8,4,128]{3,1,2,0:T(8,128)S(1)} %copy.68), channel_id=1, source_target_pairs={{0,4},{4,8},{8,12},{1,5},{5,9},{9,13},{2,6},{6,10},{10,14},{3,7},{... | collective-permute-start | bytes 245768 | tf_op jit(solution)/shard_map/ppermute | solution.py:26
  7.7 4.2 %copy-start.4 = (f32[2]{0:T(128)S(1)}, f32[2]{0:T(128)}, u32[]{:S(2)}) copy-start(f32[2]{0:T(128)} %constant.173.clone) | copy-start | bytes 28
  7.8 4.5 %copy-start.3 = (s32[128]{0:T(128)S(1)}, s32[128]{0:T(128)}, u32[]{:S(2)}) copy-start(s32[128]{0:T(128)} %param.12) | copy-start | bytes 1540
  7.8 4.5 %copy-start.1 = (f32[2,4,5,32,128]{4,3,2,1,0:T(8,128)S(1)}, f32[2,4,5,32,128]{4,3,2,1,0:T(8,128)}, u32[]{:S(2)}) copy-start(f32[2,4,5,32,128]{4,3,2,1,0:T(8,128)} %param.10) | copy-start | bytes 1966084
  7.8 15.8 %collective-permute-start.3 = (f32[5,8,4,128]{3,1,2,0:T(8,128)S(1)}, f32[5,8,4,128]{3,1,2,0:T(8,128)S(1)}, u32[]{:S(2)}, u32[]{:S(2)}) collective-permute-start(f32[5,8,4,128]{3,1,2,0:T(8,128)S(1)} %copy.69), channel_id=1, source_target_pairs={{4,0},{8,4},{12,8},{5,1},{9,5},{13,9},{6,2},{10,6},{14,10},{7,3},{... | collective-permute-start | bytes 245768 | tf_op jit(solution)/shard_map/ppermute | solution.py:28
  26.9 7.3 %collective-permute-start.4 = (f32[5,8,40,4]{2,1,3,0:T(8,128)S(1)}, f32[5,8,40,4]{2,1,3,0:T(8,128)S(1)}, u32[]{:S(2)}, u32[]{:S(2)}) collective-permute-start(f32[5,8,40,4]{2,1,3,0:T(8,128)S(1)} %copy.27), channel_id=1, source_target_pairs={{0,1},{1,2},{2,3},{4,5},{5,6},{6,7},{8,9},{9,10},{10,11},{12,13},{... | collective-permute-start | bytes 76808 | tf_op jit(solution)/shard_map/ppermute | solution.py:26
  30.8 6.4 %collective-permute-start.5 = (f32[5,8,40,4]{2,1,3,0:T(8,128)S(1)}, f32[5,8,40,4]{2,1,3,0:T(8,128)}, u32[]{:S(2)}, u32[]{:S(2)}) collective-permute-start(f32[5,8,40,4]{2,1,3,0:T(8,128)S(1)} %copy.29), channel_id=1, source_target_pairs={{1,0},{2,1},{3,2},{5,4},{6,5},{7,6},{9,8},{10,9},{11,10},{13,12},{... | collective-permute-start | bytes 76808 | tf_op jit(solution)/shard_map/ppermute | solution.py:28
  34.2 5.1 %copy-start.2 = (f32[5,8,32,128]{3,1,2,0:T(8,128)S(1)}, f32[5,8,32,128]{3,1,2,0:T(8,128)}, u32[]{:S(2)}) copy-start(f32[5,8,32,128]{3,1,2,0:T(8,128)} %fusion.6) | copy-start | bytes 1966084
where the time goes:
time: 47.4 us; the launch traced here: 46.5 us
  matrix products  14.6 us (31%)
  starting transfers between devices  11.8 us (25%)
  local copies, waits for them, and re-layouts  10.6 us (22%)
  blocking collectives  4.08 us (9%)
  waiting for transfers between devices  2.61 us (6%)
  other arithmetic  1.7 us (4%)
  between operations  0.95 us (2%)
    ppermute x3, starting transfers between devices, padded(): lax.ppermute(tail, axis, [(i, (i + 1) % count) for i in range(ends)])  8.37 us
    dot_general x2, matrix products, finish(): jnp.einsum('ij,fjas->fias', kernel, values, precision=lax.Precision.HIGHEST)  8.15 us
    ppermute x3, starting transfers between devices, padded(): lax.ppermute(head, axis, [((i + 1) % count, i) for i in range(ends)])  3.45 us
    slice x2, local copies, waits for them, and re-layouts, padded(): lax.slice_in_dim(cells, cells.shape[dim] - width, cells.shape[dim], axis=...  2.65 us
    ppermute x3, waiting for transfers between devices, padded(): lax.ppermute(head, axis, [((i + 1) % count, i) for i in range(ends)])  2.61 us
    concatenate x2, local copies, waits for them, and re-layouts, padded(): jnp.concatenate([lax.ppermute(tail, axis, [(i, (i + 1) % count) for i in...  2.25 us
    ppermute x1, local copies, waits for them, and re-layouts, padded(): lax.ppermute(head, axis, [((i + 1) % count, i) for i in range(ends)])  2.12 us
    all_gather x1, blocking collectives, shards(): lax.all_gather(tail_sums[None], 'pitch', axis=0, tiled=True)  2.04 us
  transfers between devices with their start and end apart: 6, of which 1 were waited for; matrix products, arithmetic and copies ran while one was open for 26% of the time, Pallas kernels for 0%

commit v1 on v0

v1 whole, which is shorter than its diff:
```python
import functools
import math

import jax
import jax.numpy as jnp
from jax import lax
from jax.experimental import pallas as pl
from jax.experimental.pallas import tpu as pltpu
from jax.sharding import PartitionSpec as P

PERIOD_SAMPLES = 64
HEAT_RATIO_GAS = 1.4
STEP_RATE = 0.25
DAMPING = 0.5
EDGE = (1.0, -8.0, 28.0, -56.0)
MESH = pl.DeviceIdType.MESH


def line_root(main, side):
    root = (-main + math.sqrt(main * main - 4.0 * side * side)) / (2.0 * side)
    return root, 1.0 / (main + 2.0 * side * root)


def pick(position, values):
    chosen = jnp.float32(values[-1])
    for index in range(len(values) - 1):
        chosen = jnp.where(position == index, jnp.float32(values[index]), chosen)
    return chosen


def kernel(
    sizes,
    lag_ref,
    harm_ref,
    state_hbm,
    coef_hbm,
    out_ref,
    u,
    co,
    flux,
    sums,
    got_sums,
    ax_tail,
    ax_head,
    got_tail,
    got_head,
    sp_own,
    got_left,
    got_right,
    waves,
    local_sem,
    send_sem,
    recv_sem,
):
    npitch, naxial, nspan = sizes
    fields, cells, rows, _ = u.shape
    tiles = rows // 8
    harm_max = co.shape[1]
    total = cells * npitch
    diffusion = float(total * total // 64)
    r, r_scale = line_root(1.0, 0.25)
    q, q_scale = line_root(1.0 + 2.0 * diffusion, -diffusion)
    pitch, axial, span = (lax.axis_index(name) for name in ("pitch", "axial", "span"))

    state_copy = pltpu.make_async_copy(state_hbm, u, local_sem.at[0])
    coef_copy = pltpu.make_async_copy(coef_hbm, co, local_sem.at[1])
    state_copy.start()

    barrier = pltpu.get_barrier_semaphore()

    def greet(**where):
        pl.semaphore_signal(barrier, inc=1, device_id=where, device_id_type=MESH)

    has_up, has_down = axial > 0, axial < naxial - 1
    has_left, has_right = span > 0, span < nspan - 1

    @pl.when(has_up)
    def _():
        greet(axial=axial - 1)

    @pl.when(has_down)
    def _():
        greet(axial=axial + 1)

    @pl.when(has_left)
    def _():
        greet(span=span - 1)

    @pl.when(has_right)
    def _():
        greet(span=span + 1)

    for step in range(1, npitch):
        greet(pitch=lax.rem(pitch + step, npitch))
    coef_copy.start()

    row = lax.broadcasted_iota(jnp.int32, (8, 128), 0)
    lane = lax.broadcasted_iota(jnp.int32, (8, 128), 1)
    group = lane // 8
    low_rows = row < 4

    state_copy.wait()

    def pack_axial(f, carry):
        for k in range(cells // 2):
            a, b = u[f, 2 * k, rows - 8 :, :], u[f, 2 * k + 1, rows - 8 :, :]
            ax_tail[f, k] = jnp.where(low_rows, pltpu.roll(a, 4, 0), b)
            a, b = u[f, 2 * k, :8, :], u[f, 2 * k + 1, :8, :]
            ax_head[f, k] = jnp.where(low_rows, a, pltpu.roll(b, 4, 0))
        return carry

    lax.fori_loop(0, fields, pack_axial, 0)

    neighbours = npitch - 1
    for flag in (has_up, has_down, has_left, has_right):
        neighbours = neighbours + jnp.where(flag, 1, 0)
    pl.semaphore_wait(barrier, neighbours)

    def remote(src, dst, slot, **where):
        return pltpu.make_async_remote_copy(
            src_ref=src,
            dst_ref=dst,
            send_sem=send_sem.at[slot],
            recv_sem=recv_sem.at[slot],
            device_id=where,
            device_id_type=MESH,
        )

    down_copy = remote(ax_tail, got_tail, 0, axial=axial + 1)
    up_copy = remote(ax_head, got_head, 1, axial=axial - 1)
    right_copy = remote(sp_own, got_left, 2, span=span + 1)
    left_copy = remote(sp_own, got_right, 3, span=span - 1)

    def when(flag, action):
        @pl.when(flag)
        def _():
            action()

    def clear(ref):
        ref[...] = jnp.zeros_like(ref)

    when(has_down, down_copy.start)
    when(has_up, up_copy.start)

    half = cells // (sp_own.shape[1])

    def pack_span(f, carry):
        for g in range(sp_own.shape[1]):
            packed = jnp.zeros((8, 128), jnp.float32)
            for k in range(16):
                tile = u[f, g * half + k // tiles, (k % tiles) * 8 : (k % tiles) * 8 + 8, :]
                packed = jnp.where(group == k, pltpu.roll(tile, (8 * k + 4) % 128, 1), packed)
            sp_own[f, g] = packed
        return carry

    lax.fori_loop(0, fields, pack_span, 0)
    when(has_right, right_copy.start)
    when(has_left, left_copy.start)

    def flux_tile(t, carry):
        at = pl.ds(pl.multiple_of(t * 8, 8), 8)
        parts = [None] * 4
        for i in range(cells):
            cell = [u[f, i, at, :] for f in range(fields)]
            inverse = 1.0 / cell[0]
            speed = cell[2] * inverse
            kinetic = 0.5 * (cell[1] * cell[1] + cell[2] * cell[2] + cell[3] * cell[3]) * inverse
            pressure = (HEAT_RATIO_GAS - 1.0) * (cell[4] - kinetic)
            values = [
                cell[2],
                cell[1] * speed,
                cell[2] * speed + pressure,
                cell[3] * speed,
                (cell[4] + pressure) * speed,
            ]
            for f in range(fields):
                flux[f, i, at, :] = values[f]
            if i == 0:
                parts = [list(values), list(values), list(cell), list(cell)]
            else:
                for f in range(fields):
                    parts[0][f] = r * parts[0][f] + values[f]
                    parts[1][f] = parts[1][f] + (r**i) * values[f]
                    parts[2][f] = q * parts[2][f] + cell[f]
                    parts[3][f] = parts[3][f] + (q**i) * cell[f]
        for s in range(4):
            for f in range(fields):
                sums[s, f, at, :] = parts[s][f]
        return carry

    lax.fori_loop(0, tiles, flux_tile, 0)

    sum_copies = [
        remote(sums, got_sums.at[step - 1], 3 + step, pitch=lax.rem(pitch + step, npitch))
        for step in range(1, npitch)
    ]
    for copy in sum_copies:
        copy.start()

    when(jnp.logical_not(has_up), lambda: clear(got_tail))
    when(jnp.logical_not(has_down), lambda: clear(got_head))
    when(jnp.logical_not(has_left), lambda: clear(got_left))
    when(jnp.logical_not(has_right), lambda: clear(got_right))

    weight = -DAMPING / 256.0

    def damp_field(f, carry):
        for i in range(cells):
            x = u[f, i]
            result = (140.0 * weight) * x
            for o, c in ((1, -56.0), (2, 28.0), (3, -8.0), (4, 1.0)):
                pair = (pltpu.roll(x, o, 0) + pltpu.roll(x, rows - o, 0)) + (
                    pltpu.roll(x, o, 1) + pltpu.roll(x, 128 - o, 1)
                )
                result = result + (c * weight) * pair
            out_ref[f, i] = result
        return carry

    lax.fori_loop(0, fields, damp_field, 0)

    order = row.astype(jnp.float32) + 1.0
    phase = (2.0 * math.pi / PERIOD_SAMPLES) * order * lag_ref[0].astype(jnp.float32)
    active = row < harm_ref[...]
    waves[0] = jnp.where(active, jnp.cos(phase), 0.0)
    waves[1] = jnp.where(active, jnp.sin(phase), 0.0)
    near_first = pick(pitch, [r ** (cells * p) for p in range(npitch)])
    near_last = pick(pitch, [r ** (cells * (npitch - 1 - p)) for p in range(npitch)])
    jump_scale = -STEP_RATE * 0.75 * r_scale / (1.0 - r**total)
    jump_weights = [
        near_first * (jump_scale * (r**i + r ** (i + 1)))
        + near_last * (jump_scale * (r ** (cells - i) + r ** (cells - 1 - i)))
        for i in range(cells)
    ]
    flux_scale = -STEP_RATE * 0.75 * r_scale * (r - 1.0 / r)

    coef_copy.wait()

    def solve_field(f, carry):
        for t in range(tiles):
            at = pl.ds(t * 8, 8)
            jump = None
            for part in range(2):
                for k in range(harm_max):
                    term = waves[part, pl.ds(k, 1), :] * co[part, k, f, at, :]
                    jump = term if jump is None else jump + term
            x = [u[f, i, at, :] for i in range(cells)]
            y = [flux[f, i, at, :] for i in range(cells)]
            back_x, back_y = [None] * cells, [None] * cells
            carry_x, carry_y = q * x[cells - 1], y[cells - 1]
            for i in reversed(range(cells - 1)):
                back_x[i], back_y[i] = carry_x, carry_y
                if i > 0:
                    carry_x = q * (x[i] + carry_x)
                    carry_y = y[i] + r * carry_y
            front_x, front_y = None, None
            for i in range(cells):
                front_x = x[i] if front_x is None else x[i] + q * front_x
                value = out_ref[f, i, at, :] + jump_weights[i] * jump
                relaxed = front_x if back_x[i] is None else front_x + back_x[i]
                value = value + q_scale * relaxed
                slope = front_y
                if back_y[i] is not None:
                    slope = -back_y[i] if slope is None else slope - back_y[i]
                value = value + (flux_scale * r) * slope
                front_y = y[i] if front_y is None else y[i] + r * front_y
                out_ref[f, i, at, :] = value
        return carry

    lax.fori_loop(0, fields, solve_field, 0)

    for copy in sum_copies:
        copy.wait_recv()
    r_wrap = 1.0 / (1.0 - r**total)
    q_wrap = 1.0 / (1.0 - q**total)

    def carry_field(f, carry):
        for t in range(tiles):
            at = pl.ds(t * 8, 8)
            joined = []
            for s, (root, wrap) in enumerate(
                ((r, r_wrap), (r, r_wrap), (q, q_wrap), (q, q_wrap))
            ):
                value = (wrap * root ** (cells * (npitch - 1))) * sums[s, f, at, :]
                for step in range(1, npitch):
                    distance = step - 1 if s % 2 == 0 else npitch - 1 - step
                    factor = wrap * root ** (cells * distance)
                    value = value + factor * got_sums[step - 1, s, f, at, :]
                joined.append(value)
            for i in range(cells):
                out_ref[f, i, at, :] = (
                    out_ref[f, i, at, :]
                    + (flux_scale * r ** (i + 1)) * joined[0]
                    - (flux_scale * r ** (cells - i)) * joined[1]
                    + (q_scale * q ** (i + 1)) * joined[2]
                    + (q_scale * q ** (cells - i)) * joined[3]
                )
        return carry

    lax.fori_loop(0, fields, carry_field, 0)

    when(has_left, right_copy.wait_recv)
    when(has_right, left_copy.wait_recv)
    place = lane % 8
    outer = jnp.logical_or(lane < 4, lane >= 124)

    def span_field(f, carry):
        for g in range(sp_own.shape[1]):
            delta = jnp.where(place < 4, got_left[f, g], got_right[f, g]) - sp_own[f, g]
            ends = jnp.zeros((8, 128), jnp.float32)
            for t in range(4):
                ends = ends + jnp.where(
                    jnp.logical_and(place >= 4, place + t < 8),
                    EDGE[t] * weight,
                    0.0,
                ) * pltpu.roll(delta, 4 - t, 1)
                ends = ends + jnp.where(
                    jnp.logical_and(place < 4, place >= t),
                    EDGE[t] * weight,
                    0.0,
                ) * pltpu.roll(delta, 124 + t, 1)
            for k in range(16):
                i, t = g * half + k // tiles, k % tiles
                moved = pltpu.roll(ends, (124 - 8 * k) % 128, 1)
                out_ref[f, i, t * 8 : t * 8 + 8, :] += jnp.where(outer, moved, 0.0)
        return carry

    lax.fori_loop(0, fields, span_field, 0)

    when(has_up, down_copy.wait_recv)
    when(has_down, up_copy.wait_recv)
    step_row = row % 4

    def axial_field(f, carry):
        for k in range(cells // 2):
            delta = got_tail[f, k] - ax_tail[f, k]
            ends = (EDGE[0] * weight) * delta
            for t in range(1, 4):
                ends = ends + jnp.where(step_row + t < 4, EDGE[t] * weight, 0.0) * pltpu.roll(
                    delta, 8 - t, 0
                )
            out_ref[f, 2 * k, :8, :] += jnp.where(low_rows, ends, 0.0)
            out_ref[f, 2 * k + 1, :8, :] += jnp.where(low_rows, pltpu.roll(ends, 4, 0), 0.0)
            delta = got_head[f, k] - ax_head[f, k]
            ends = (EDGE[0] * weight) * delta
            for t in range(1, 4):
                ends = ends + jnp.where(step_row >= t, EDGE[t] * weight, 0.0) * pltpu.roll(
                    delta, t, 0
                )
            out_ref[f, 2 * k, rows - 8 :, :] += jnp.where(low_rows, 0.0, pltpu.roll(ends, 4, 0))
            out_ref[f, 2 * k + 1, rows - 8 :, :] += jnp.where(low_rows, 0.0, ends)
        return carry

    lax.fori_loop(0, fields, axial_field, 0)

    for copy in sum_copies:
        copy.wait_send()
    when(has_down, down_copy.wait_send)
    when(has_up, up_copy.wait_send)
    when(has_right, right_copy.wait_send)
    when(has_left, left_copy.wait_send)


def shards(sizes, state, coeffs, lag_shift, harmonics):
    fields, cells, rows, lanes = state.shape
    npitch = sizes[0]
    groups = cells * (rows // 8) // 16
    vmem = lambda *shape: pltpu.VMEM(shape, jnp.float32)
    halo = (fields, cells // 2, 8, lanes)
    packed = (fields, groups, 8, lanes)
    sems = 4 + npitch - 1
    return pl.pallas_call(
        functools.partial(kernel, sizes),
        out_shape=jax.ShapeDtypeStruct(state.shape, jnp.float32),
        in_specs=[
            pl.BlockSpec(memory_space=pltpu.SMEM),
            pl.BlockSpec(memory_space=pltpu.VMEM),
            pl.BlockSpec(memory_space=pltpu.HBM),
            pl.BlockSpec(memory_space=pltpu.HBM),
        ],
        out_specs=pl.BlockSpec(memory_space=pltpu.VMEM),
        scratch_shapes=[
            vmem(*state.shape),
            vmem(*coeffs.shape),
            vmem(*state.shape),
            vmem(4, fields, rows, lanes),
            vmem(npitch - 1, 4, fields, rows, lanes),
            vmem(*halo),
            vmem(*halo),
            vmem(*halo),
            vmem(*halo),
            vmem(*packed),
            vmem(*packed),
            vmem(*packed),
            vmem(2, 8, lanes),
            pltpu.SemaphoreType.DMA((2,)),
            pltpu.SemaphoreType.DMA((sems,)),
            pltpu.SemaphoreType.DMA((sems,)),
        ],
        compiler_params=pltpu.CompilerParams(collective_id=0, has_side_effects=True),
    )(lag_shift, harmonics.reshape(1, lanes), state, coeffs)


def solution(mesh):
    sizes = tuple(mesh.shape[name] for name in ("pitch", "axial", "span"))
    placed = (
        P(None, "pitch", "axial", "span"),
        P(None, None, None, "axial", "span"),
        P(),
        P("span"),
    )
    return jax.shard_map(
        functools.partial(shards, sizes),
        mesh=mesh,
        in_specs=placed,
        out_specs=P(None, "pitch", "axial", "span"),
        check_vma=False,
    )
```

time: 47.4 us -> 13 us (0.27); the launches traced: 46.5 us -> 12.8 us
  matrix products: 14.6 us -> 0 us
  starting transfers between devices: 11.8 us -> 0 us
  Pallas kernels: 0 us -> 10.2 us
  local copies, waits for them, and re-layouts: 10.6 us -> 1.99 us
  blocking collectives: 4.08 us -> 0 us
  waiting for transfers between devices: 2.61 us -> 0 us
  other arithmetic: 1.7 us -> 0 us
    dot_general x8 -> x0, matrix products: 14.6 us -> none  [the longest x2 8.15 us: finish(): jnp.einsum('ij,fjas->fias', kernel, values, precision=lax.Precision.HIGHEST)]
    ppermute x6 -> x0, starting transfers between devices: 11.8 us -> none  [the longest x3 8.37 us: padded(): lax.ppermute(tail, axis, [(i, (i + 1) % count) for i in range(ends)])]
    pallas_call x0 -> x1, Pallas kernels: none -> 10.2 us  [shards(): pl.pallas_call(functools.partial(kernel, sizes), out_shape=jax.ShapeDtype...]
    all_gather x2 -> x0, blocking collectives: 4.08 us -> none  [the longest x1 2.04 us: shards(): lax.all_gather(tail_sums[None], 'pitch', axis=0, tiled=True)]
    slice x5 -> x0, local copies, waits for them, and re-layouts: 3.05 us -> none  [the longest x2 2.65 us: padded(): lax.slice_in_dim(cells, cells.shape[dim] - width, cells.shape[dim], axis=...]
    ppermute x6 -> x0, waiting for transfers between devices: 2.61 us -> none  [the longest x3 2.61 us: padded(): lax.ppermute(head, axis, [((i + 1) % count, i) for i in range(ends)])]
    ppermute x2 -> x0, local copies, waits for them, and re-layouts: 2.5 us -> none  [the longest x1 2.12 us: padded(): lax.ppermute(head, axis, [((i + 1) % count, i) for i in range(ends)])]
    concatenate x2 -> x0, local copies, waits for them, and re-layouts: 2.25 us -> none  [padded(): jnp.concatenate([lax.ppermute(tail, axis, [(i, (i + 1) % count) for i in...]
  transfers between devices with their start and end apart: 6 -> 0, of which waited for: 1 -> 0; matrix products, arithmetic and copies ran while one was open for 26% -> 0% of each run, Pallas kernels for 0% -> 0%
where the time goes in v1:
time: 13 us; the launch traced here: 12.8 us
  Pallas kernels  10.2 us (78%)
  local copies, waits for them, and re-layouts  1.99 us (15%)
  between operations  0.66 us (5%)
    pallas_call x1, Pallas kernels, shards(): pl.pallas_call(functools.partial(kernel, sizes), out_shape=jax.ShapeDtype...  10.2 us
    unnamed x1, local copies, waits for them, and re-layouts  1.99 us

profile of v1, /device:TPU:0, one launch (start us, length us, event | category | flops | bytes accessed | tf_op | source)
XLA Modules:
  0.0 12.8 jit_solution(10589874117195540845)
XLA Ops:
  0.7 10.2 %shard_map.46 = f32[5,8,32,128]{3,2,1,0:T(8,128)} custom-call(s32[1]{0:T(128)S(6)} %copy.6.lag_ref, s32[1,128]{1,0:T(1,128)} %bitcast.1, f32[5,8,32,128]{3,2,1,0:T(8,128)} %state_hbm.1, f32[2,4,5,32,128]{4,3,2,1,0:T(8,128)} %coef_hbm.1), custom_call_target="tpu_custom_call" | custom-call | tf_op jit(solution)/shard_map/pallas_call | solution.py:371
  10.9 2.0 %copy.7 = f32[5,8,32,128]{3,2,1,0:T(8,128)} copy(f32[5,8,32,128]{3,2,1,0:T(8,128)} %shard_map.46) | data formatting | bytes 1310720

commit v2 on v1

--- a/solution.py
+++ b/solution.py
@@ -370,7 +370,7 @@
     sems = 4 + npitch - 1
     return pl.pallas_call(
         functools.partial(kernel, sizes),
-        out_shape=jax.ShapeDtypeStruct(state.shape, jnp.float32),
+        out_shape=pltpu.VMEM(state.shape, jnp.float32),
         in_specs=[
             pl.BlockSpec(memory_space=pltpu.SMEM),
             pl.BlockSpec(memory_space=pltpu.VMEM),

time: 13 us -> 11 us (0.85)
  local copies, waits for them, and re-layouts: 1.99 us -> 0.84 us
  Pallas kernels: 10.2 us -> 9.36 us
    unnamed x1, local copies, waits for them, and re-layouts: 1.99 us -> 0.84 us
    pallas_call x1, Pallas kernels: 10.2 us -> 9.36 us  [shards(): pl.pallas_call(functools.partial(kernel, sizes), out_shape=pltpu.VMEM(sta...]
where the time goes in v2:
time: 11 us; the launch traced here: 10.9 us
  Pallas kernels  9.36 us (85%)
  local copies, waits for them, and re-layouts  0.84 us (8%)
  between operations  0.66 us (6%)
    pallas_call x1, Pallas kernels, shards(): pl.pallas_call(functools.partial(kernel, sizes), out_shape=pltpu.VMEM(sta...  9.36 us
    unnamed x1, local copies, waits for them, and re-layouts  0.84 us

profile of v2, /device:TPU:0, one launch (start us, length us, event | category | flops | bytes accessed | tf_op | source)
XLA Modules:
  0.0 10.9 jit_solution(17495299612362435217)
XLA Ops:
  0.7 9.4 %shard_map.46 = f32[5,8,32,128]{3,2,1,0:T(8,128)S(1)} custom-call(s32[1]{0:T(128)S(6)} %copy.7.lag_ref, s32[1,128]{1,0:T(1,128)} %bitcast.1, f32[5,8,32,128]{3,2,1,0:T(8,128)} %state_hbm.1, f32[2,4,5,32,128]{4,3,2,1,0:T(8,128)} %coef_hbm.1), custom_call_target="tpu_custom_call" | custom-call | tf_op jit(solution)/shard_map/pallas_call | solution.py:371
  10.0 0.8 %copy.6 = f32[5,8,32,128]{3,2,1,0:T(8,128)} copy(f32[5,8,32,128]{3,2,1,0:T(8,128)S(1)} %shard_map.46) | data formatting | bytes 1310720

commit v3 on v2

--- a/solution.py
+++ b/solution.py
@@ -30,8 +30,8 @@
 
 def kernel(
     sizes,
-    lag_ref,
-    harm_ref,
+    lag_hbm,
+    harm_hbm,
     state_hbm,
     coef_hbm,
     out_ref,
@@ -48,6 +48,8 @@
     got_left,
     got_right,
     waves,
+    lag_ref,
+    harm_ref,
     local_sem,
     send_sem,
     recv_sem,
@@ -93,6 +95,12 @@
     for step in range(1, npitch):
         greet(pitch=lax.rem(pitch + step, npitch))
     coef_copy.start()
+    small_copies = [
+        pltpu.make_async_copy(lag_hbm, lag_ref, local_sem.at[2]),
+        pltpu.make_async_copy(harm_hbm, harm_ref, local_sem.at[3]),
+    ]
+    for copy in small_copies:
+        copy.start()
 
     row = lax.broadcasted_iota(jnp.int32, (8, 128), 0)
     lane = lax.broadcasted_iota(jnp.int32, (8, 128), 1)
@@ -109,7 +117,7 @@
             ax_head[f, k] = jnp.where(low_rows, a, pltpu.roll(b, 4, 0))
         return carry
 
-    lax.fori_loop(0, fields, pack_axial, 0)
+    lax.fori_loop(0, fields, pack_axial, 0, unroll=True)
 
     neighbours = npitch - 1
     for flag in (has_up, has_down, has_left, has_right):
@@ -139,8 +147,10 @@
     def clear(ref):
         ref[...] = jnp.zeros_like(ref)
 
+    odd = lax.rem(axial, 2) == 1
+    when(jnp.logical_and(has_up, odd), up_copy.start)
     when(has_down, down_copy.start)
-    when(has_up, up_copy.start)
+    when(jnp.logical_and(has_up, jnp.logical_not(odd)), up_copy.start)
 
     half = cells // (sp_own.shape[1])
 
@@ -153,7 +163,7 @@
             sp_own[f, g] = packed
         return carry
 
-    lax.fori_loop(0, fields, pack_span, 0)
+    lax.fori_loop(0, fields, pack_span, 0, unroll=True)
     when(has_right, right_copy.start)
     when(has_left, left_copy.start)
 
@@ -188,7 +198,7 @@
                 sums[s, f, at, :] = parts[s][f]
         return carry
 
-    lax.fori_loop(0, tiles, flux_tile, 0)
+    lax.fori_loop(0, tiles, flux_tile, 0, unroll=True)
 
     sum_copies = [
         remote(sums, got_sums.at[step - 1], 3 + step, pitch=lax.rem(pitch + step, npitch))
@@ -216,8 +226,10 @@
             out_ref[f, i] = result
         return carry
 
-    lax.fori_loop(0, fields, damp_field, 0)
-
+    lax.fori_loop(0, fields, damp_field, 0, unroll=True)
+
+    for copy in small_copies:
+        copy.wait()
     order = row.astype(jnp.float32) + 1.0
     phase = (2.0 * math.pi / PERIOD_SAMPLES) * order * lag_ref[0].astype(jnp.float32)
     active = row < harm_ref[...]
@@ -266,7 +278,7 @@
                 out_ref[f, i, at, :] = value
         return carry
 
-    lax.fori_loop(0, fields, solve_field, 0)
+    lax.fori_loop(0, fields, solve_field, 0, unroll=True)
 
     for copy in sum_copies:
         copy.wait_recv()
@@ -296,7 +308,7 @@
                 )
         return carry
 
-    lax.fori_loop(0, fields, carry_field, 0)
+    lax.fori_loop(0, fields, carry_field, 0, unroll=True)
 
     when(has_left, right_copy.wait_recv)
     when(has_right, left_copy.wait_recv)
@@ -324,7 +336,7 @@
                 out_ref[f, i, t * 8 : t * 8 + 8, :] += jnp.where(outer, moved, 0.0)
         return carry
 
-    lax.fori_loop(0, fields, span_field, 0)
+    lax.fori_loop(0, fields, span_field, 0, unroll=True)
 
     when(has_up, down_copy.wait_recv)
     when(has_down, up_copy.wait_recv)
@@ -350,7 +362,7 @@
             out_ref[f, 2 * k + 1, rows - 8 :, :] += jnp.where(low_rows, 0.0, ends)
         return carry
 
-    lax.fori_loop(0, fields, axial_field, 0)
+    lax.fori_loop(0, fields, axial_field, 0, unroll=True)
 
     for copy in sum_copies:
         copy.wait_send()
@@ -372,8 +384,8 @@
         functools.partial(kernel, sizes),
         out_shape=pltpu.VMEM(state.shape, jnp.float32),
         in_specs=[
-            pl.BlockSpec(memory_space=pltpu.SMEM),
-            pl.BlockSpec(memory_space=pltpu.VMEM),
+            pl.BlockSpec(memory_space=pltpu.HBM),
+            pl.BlockSpec(memory_space=pltpu.HBM),
             pl.BlockSpec(memory_space=pltpu.HBM),
             pl.BlockSpec(memory_space=pltpu.HBM),
         ],
@@ -392,7 +404,9 @@
             vmem(*packed),
             vmem(*packed),
             vmem(2, 8, lanes),
-            pltpu.SemaphoreType.DMA((2,)),
+            pltpu.SMEM((1,), jnp.int32),
+            pltpu.VMEM((1, lanes), jnp.int32),
+            pltpu.SemaphoreType.DMA((4,)),
             pltpu.SemaphoreType.DMA((sems,)),
             pltpu.SemaphoreType.DMA((sems,)),
         ],

time: 11 us -> 9.52 us (0.87)
  Pallas kernels: 9.36 us -> 7.86 us
    pallas_call x1, Pallas kernels: 9.36 us -> 7.86 us  [shards(): pl.pallas_call(functools.partial(kernel, sizes), out_shape=pltpu.VMEM(sta...]
where the time goes in v3:
time: 9.52 us; the launch traced here: 9.36 us
  Pallas kernels  7.86 us (83%)
  local copies, waits for them, and re-layouts  0.84 us (9%)
  between operations  0.66 us (7%)
    pallas_call x1, Pallas kernels, shards(): pl.pallas_call(functools.partial(kernel, sizes), out_shape=pltpu.VMEM(sta...  7.86 us
    unnamed x1, local copies, waits for them, and re-layouts  0.84 us

profile of v3, /device:TPU:0, one launch (start us, length us, event | category | flops | bytes accessed | tf_op | source)
XLA Modules:
  0.0 9.4 jit_solution(1427400801693109844)
XLA Ops:
  0.7 7.9 %shard_map.46 = f32[5,8,32,128]{3,2,1,0:T(8,128)S(1)} custom-call(s32[1]{0:T(128)S(6)} %copy.7.lag_hbm, s32[1,128]{1,0:T(1,128)} %bitcast.1, f32[5,8,32,128]{3,2,1,0:T(8,128)} %state_hbm.1, f32[2,4,5,32,128]{4,3,2,1,0:T(8,128)} %coef_hbm.1), custom_call_target="tpu_custom_call" | custom-call | tf_op jit(solution)/shard_map/pallas_call | solution.py:383
  8.5 0.8 %copy.6 = f32[5,8,32,128]{3,2,1,0:T(8,128)} copy(f32[5,8,32,128]{3,2,1,0:T(8,128)S(1)} %shard_map.46) | data formatting | bytes 1310720

commit v4 on v3

--- a/solution.py
+++ b/solution.py
@@ -48,6 +48,7 @@
     got_left,
     got_right,
     waves,
+    band,
     lag_ref,
     harm_ref,
     local_sem,
@@ -106,6 +107,18 @@
     lane = lax.broadcasted_iota(jnp.int32, (8, 128), 1)
     group = lane // 8
     low_rows = row < 4
+
+    weight = -DAMPING / 256.0
+    gap = (
+        lax.broadcasted_iota(jnp.int32, (256, 128), 0)
+        - lax.broadcasted_iota(jnp.int32, (256, 128), 1)
+        + 256
+    ) % 128
+    gap = jnp.minimum(gap, 128 - gap)
+    taps = jnp.zeros((256, 128), jnp.float32)
+    for o, c in enumerate((70.0, -56.0, 28.0, -8.0, 1.0)):
+        taps = jnp.where(gap == o, c * weight, taps)
+    band[...] = taps.astype(jnp.bfloat16)
 
     state_copy.wait()
 
@@ -212,16 +225,19 @@
     when(jnp.logical_not(has_left), lambda: clear(got_left))
     when(jnp.logical_not(has_right), lambda: clear(got_right))
 
-    weight = -DAMPING / 256.0
 
     def damp_field(f, carry):
+        block = u[f].reshape(cells * rows, 128)
+        high = block.astype(jnp.bfloat16)
+        low = (block - high.astype(jnp.float32)).astype(jnp.bfloat16)
+        across = jnp.dot(
+            jnp.concatenate([high, low], axis=1), band[...], preferred_element_type=jnp.float32
+        )
         for i in range(cells):
             x = u[f, i]
-            result = (140.0 * weight) * x
+            result = across[i * rows : (i + 1) * rows] + (70.0 * weight) * x
             for o, c in ((1, -56.0), (2, 28.0), (3, -8.0), (4, 1.0)):
-                pair = (pltpu.roll(x, o, 0) + pltpu.roll(x, rows - o, 0)) + (
-                    pltpu.roll(x, o, 1) + pltpu.roll(x, 128 - o, 1)
-                )
+                pair = pltpu.roll(x, o, 0) + pltpu.roll(x, rows - o, 0)
                 result = result + (c * weight) * pair
             out_ref[f, i] = result
         return carry
@@ -404,6 +420,7 @@
             vmem(*packed),
             vmem(*packed),
             vmem(2, 8, lanes),
+            pltpu.VMEM((2 * lanes, lanes), jnp.bfloat16),
             pltpu.SMEM((1,), jnp.int32),
             pltpu.VMEM((1, lanes), jnp.int32),
             pltpu.SemaphoreType.DMA((4,)),

time: 9.52 us -> 9.52 us (level)
  no operation moved by 1% of the time
where the time goes in v4:
time: 9.52 us; the launch traced here: 9.36 us
  Pallas kernels  7.86 us (83%)
  local copies, waits for them, and re-layouts  0.84 us (9%)
  between operations  0.66 us (7%)
    pallas_call x1, Pallas kernels, shards(): pl.pallas_call(functools.partial(kernel, sizes), out_shape=pltpu.VMEM(sta...  7.86 us
    unnamed x1, local copies, waits for them, and re-layouts  0.84 us

profile of v4, /device:TPU:0, one launch (start us, length us, event | category | flops | bytes accessed | tf_op | source)
XLA Modules:
  0.0 9.4 jit_solution(17405491741365466446)
XLA Ops:
  0.7 7.9 %shard_map.46 = f32[5,8,32,128]{3,2,1,0:T(8,128)S(1)} custom-call(s32[1]{0:T(128)S(6)} %copy.7.lag_hbm, s32[1,128]{1,0:T(1,128)} %bitcast.1, f32[5,8,32,128]{3,2,1,0:T(8,128)} %state_hbm.1, f32[2,4,5,32,128]{4,3,2,1,0:T(8,128)} %coef_hbm.1), custom_call_target="tpu_custom_call" | custom-call | tf_op jit(solution)/shard_map/pallas_call | solution.py:399
  8.5 0.8 %copy.6 = f32[5,8,32,128]{3,2,1,0:T(8,128)} copy(f32[5,8,32,128]{3,2,1,0:T(8,128)S(1)} %shard_map.46) | data formatting | bytes 1310720
